TPU v7x, 32 devices: a whole 2x2x4 slice. The times are simulated.
32 devices in a mesh: row: 8 (over z, y), col: 4 (over x, core).
Axes of the slice: x: 2, y: 2, z: 4, core: 2. Of those that a mesh axis runs over, the one named last changes fastest.
Arguments:
- candidates: float32 [512, 32768], P('col', 'row'), may hold values from -64 to 64
- trailing: float32 [512, 32768], P('col', 'row'), may hold values from -64 to 64
- pivots: int32 [64], replicated, may hold values from 0 to 511, as said below
Outputs:
- r_panel: float32 [64, 64], replicated
- r_trail: float32 [64, 512], P(None, 'col')
- basis: float32 [64, 32768], P(None, 'row')
- trailing_next: float32 [512, 32768], P('col', 'row')
Inputs may be any that keep to these rules, and one draw needn't show every extreme that they name: `pivots`: 64 distinct column numbers; one block of 128 consecutive columns (those of one index of col) holds exactly 32 of them and no block holds more.
All inputs are finite; a program needn't handle non-finite values.
Results may differ from a plain program's by a relative error of at most 0.0003.
Values sent between devices are 32-bit elements; how exact they have to be, the bound alone decides.
A program may use at most 64 MiB of HBM per device.

v0:
```python
import functools

import jax
import jax.numpy as jnp
from jax import lax
from jax.experimental import pallas as pl
from jax.experimental.pallas import tpu as pltpu
from jax.sharding import PartitionSpec as P

MESH = pl.DeviceIdType.MESH
CORES = 2
F32 = jnp.float32
BF16 = jnp.bfloat16
BLOCK = 16
PIECES = (1, 4, 3)
UPDATE_CHUNKS = 4


def split(x):
    high = x.astype(BF16)
    return high, (x - high.astype(F32)).astype(BF16)


def dot(a, b):
    return jnp.dot(a, b, preferred_element_type=F32)


def dot_t(a, b):
    return lax.dot_general(a, b, (((1,), (1,)), ((), ())), preferred_element_type=F32)


def iota(shape, dim):
    return lax.broadcasted_iota(jnp.int32, shape, dim)


def eliminate(state, start):
    rest = state
    tile = iota((BLOCK, state.shape[1]), 0)
    columns = [jnp.broadcast_to(rest[:, start + c:start + c + 1], rest.shape) for c in range(BLOCK)]
    for c in range(BLOCK):
        inverse = 1.0 / columns[c][c:c + 1]
        below = jnp.where(tile > c, columns[c][:BLOCK], 0.0)
        if rest.shape[0] > BLOCK:
            below = jnp.concatenate([below, columns[c][BLOCK:]], axis=0)
        for e in range(c + 1, BLOCK):
            columns[e] = columns[e] - below * (columns[e][c:c + 1] * inverse)
        rest = rest - below * (rest[c:c + 1] * inverse)
    return rest[:BLOCK], rest[BLOCK:]


def gather_kernel(
    n_row, n_col, windows,
    piv_ref, cand_hbm, trail_hbm,
    factor_ref, inverse_ref, cross_ref, high_hbm, low_hbm,
    cand, trail, high_ref, low_ref, bufs, grams, csend, crecv, cfull,
    cand_sem, trail_sem, panel_sem,
    xs, xr, ss, sr, fs, fr, gs, gr, cs, cr, as_, ar,
    up_sem, down_sem, mate_sem,
):
    row = lax.axis_index("row")
    col = lax.axis_index("col")
    n_x = n_col // CORES
    x = col // CORES
    core = lax.rem(col, CORES)
    sibling = x * CORES + (1 - core)
    count = piv_ref.shape[1]
    cap = count // 2
    cand_count = cand.shape[0]

    def x_peer(d):
        return lax.rem(x + d, n_x) * CORES + core

    def x_source(d):
        return lax.rem(x + n_x - d, n_x) * CORES + core

    def row_peer(d):
        return lax.rem(row + d, n_row)

    cand_copies = []
    for k, (first, width) in enumerate(windows):
        window = pl.ds(first, width)
        copy = pltpu.make_async_copy(cand_hbm.at[:, window], cand.at[:, window], cand_sem.at[k])
        copy.start()
        cand_copies.append(copy)
    trail_copy = pltpu.make_async_copy(trail_hbm, trail, trail_sem)

    barrier = pltpu.get_barrier_semaphore()
    pl.semaphore_signal(barrier, inc=1, device_id=(row, sibling), device_id_type=MESH)
    for d in range(1, n_x):
        pl.semaphore_signal(barrier, inc=1, device_id=(row, x_peer(d)), device_id_type=MESH)
    mate = row + 1 - 2 * lax.rem(row, 2)
    has_below, has_above = row >= 2, row < n_row - 2

    def signal(semaphore, to):
        pl.semaphore_signal(semaphore, inc=1, device_id=(to, col), device_id_type=MESH)

    signal(barrier, mate)
    pl.when(has_below)(lambda: signal(barrier, row - 2))
    pl.when(has_above)(lambda: signal(barrier, row + 2))

    piv_lane = jnp.broadcast_to(piv_ref[...].astype(F32), (count, count))
    rows_i, lanes_i = iota((count, count), 0), iota((count, count), 1)
    piv_sub = jnp.sum(jnp.where(rows_i == lanes_i, piv_lane, 0.0), axis=1, keepdims=True)
    owner_lane = jnp.zeros((count, count), F32)
    owner_sub = jnp.zeros((count, 1), F32)
    for s in range(1, n_col):
        owner_lane += (piv_lane >= s * cand_count).astype(F32)
        owner_sub += (piv_sub >= s * cand_count).astype(F32)
    same = jnp.broadcast_to(owner_sub, (count, count)) == owner_lane
    rank_sub = jnp.sum(jnp.where(same & (lanes_i < rows_i), 1.0, 0.0), axis=1, keepdims=True)
    rank_lane = jnp.sum(jnp.where(same & (rows_i < lanes_i), 1.0, 0.0), axis=0, keepdims=True)
    slot_sub = (owner_sub * cap + rank_sub).astype(jnp.int32)
    slot_lane = (owner_lane[:1] * cap + rank_lane).astype(jnp.int32)
    expand = (slot_sub == iota((count, n_col * cap), 1)).astype(F32).astype(BF16)
    to_slot = (slot_lane == col * cap + iota((cap, count), 0)).astype(F32).astype(BF16)
    to_cand = (piv_sub.astype(jnp.int32) == col * cand_count + iota((count, cand_count), 1))
    pick = dot(to_slot, to_cand.astype(F32).astype(BF16)).astype(BF16)

    def remote(src, dst, send, recv, device):
        return pltpu.make_async_remote_copy(
            src_ref=src, dst_ref=dst, send_sem=send, recv_sem=recv,
            device_id=device, device_id_type=MESH,
        )

    sends = []
    for k, (first, width) in enumerate(windows):
        window = pl.ds(first, width)
        cand_copies[k].wait()
        high, low = split(cand[:, window])
        bufs[col, :, window] = dot(pick, high) + dot(pick, low)
        if k == 0:
            pl.semaphore_wait(barrier, n_x + 1 + has_below.astype(jnp.int32) + has_above.astype(jnp.int32))
        mine = bufs.at[col, :, window]
        for d in range(1, n_x):
            copy = remote(mine, mine, xs.at[k, d - 1], xr.at[k, d - 1], (row, x_peer(d)))
            copy.start()
            sends.append(copy)
        copy = remote(mine, mine, ss.at[k], sr.at[k], (row, sibling))
        copy.start()
        sends.append(copy)

    trail_copy.start()
    @pl.when(jnp.logical_not(has_below))
    def _():
        signal(up_sem, row + 2)

    @pl.when(jnp.logical_not(has_above))
    def _():
        signal(down_sem, row - 2)

    @pl.when(has_below)
    def _():
        pl.semaphore_wait(up_sem, 1)
        pl.when(has_above)(lambda: signal(up_sem, row + 2))

    @pl.when(has_above)
    def _():
        pl.semaphore_wait(down_sem, 1)
        pl.when(has_below)(lambda: signal(down_sem, row - 2))

    signal(mate_sem, mate)
    tc = trail.shape[0]
    acc = jnp.zeros((count, count + tc), F32)
    stores = []
    trail_copy.wait()
    for k, (first, width) in enumerate(windows):
        window = pl.ds(first, width)
        for d in range(1, n_x):
            theirs = bufs.at[x_source(d), :, window]
            remote(theirs, theirs, xs.at[k, d - 1], xr.at[k, d - 1], (row, x_peer(d))).wait_recv()
            copy = remote(theirs, theirs, fs.at[k, d - 1], fr.at[k, d - 1], (row, sibling))
            copy.start()
            sends.append(copy)
        t_high, t_low = split(trail[:, window])
        arrived = bufs.at[sibling, :, window]
        remote(arrived, arrived, ss.at[k], sr.at[k], (row, sibling)).wait_recv()
        for d in range(1, n_x):
            arrived = bufs.at[lax.rem(x + n_x - d, n_x) * CORES + (1 - core), :, window]
            remote(arrived, arrived, fs.at[k, d - 1], fr.at[k, d - 1], (row, sibling)).wait_recv()
        high, low = split(bufs[:, :, window].reshape(n_col * cap, width))
        p_high = dot(expand, high).astype(BF16)
        p_low = dot(expand, low).astype(BF16)
        high_ref[:, window] = p_high
        low_ref[:, window] = p_low
        for i, (src, dst) in enumerate(((high_ref, high_hbm), (low_ref, low_hbm))):
            copy = pltpu.make_async_copy(src.at[:, window], dst.at[:, window], panel_sem.at[k, i])
            copy.start()
            stores.append(copy)
        both = dot_t(jnp.concatenate([p_high, p_low], axis=0), jnp.concatenate([p_high, t_high], axis=0))
        acc += both[:count] + both[count:] + dot_t(p_high, jnp.concatenate([p_low, t_low], axis=0))

    pl.semaphore_wait(mate_sem, 1)
    part = count // n_row
    half = count // 2
    for r in range(n_row):
        csend[r] = acc[r * part:(r + 1) * part, count:]
    crecv[row] = csend[row]
    for d in range(1, n_row):
        copy = remote(csend.at[row_peer(d)], crecv.at[row], cs.at[d - 1], cr.at[d - 1], (row_peer(d), col))
        copy.start()
        sends.append(copy)

    grams[row] = jnp.concatenate([acc[:half, :count], acc[half:, :count]], axis=1)
    for d in range(1, n_row):
        mine = grams.at[row]
        copy = remote(mine, mine, gs.at[d - 1], gr.at[d - 1], (row_peer(d), col))
        copy.start()
        sends.append(copy)
    def source(d):
        return lax.rem(row + n_row - d, n_row)

    for d in range(1, n_row):
        arrived = crecv.at[source(d)]
        remote(arrived, arrived, cs.at[d - 1], cr.at[d - 1], (row_peer(d), col)).wait_recv()
    cfull[row] = jnp.sum(crecv[...], axis=0)
    for d in range(1, n_row):
        mine = cfull.at[row]
        copy = remote(mine, mine, as_.at[d - 1], ar.at[d - 1], (row_peer(d), col))
        copy.start()
        sends.append(copy)
    for d in range(1, n_row):
        arrived = grams.at[source(d)]
        remote(arrived, arrived, gs.at[d - 1], gr.at[d - 1], (row_peer(d), col)).wait_recv()
    packed = jnp.sum(grams[...], axis=0)
    gram = jnp.concatenate([packed[:, :count], packed[:, count:]], axis=0)
    unit = jnp.where(rows_i == lanes_i, 1.0, 0.0)
    state = jnp.concatenate([gram, unit], axis=1)
    done = []
    for start in range(0, count, BLOCK):
        block, state = eliminate(state, start)
        done.append(block)
    state = jnp.concatenate(done, axis=0)
    wide = (count, 2 * count)
    diagonal = jnp.sum(jnp.where(iota(wide, 0) == iota(wide, 1), state, 0.0), axis=1, keepdims=True)
    scaled = state / jnp.sqrt(diagonal)
    factor_ref[...] = jnp.where(iota(wide, 0) <= iota(wide, 1), scaled, 0.0)[:, :count]
    inverse_ref[...] = scaled[:, count:]
    for d in range(1, n_row):
        arrived = cfull.at[source(d)]
        remote(arrived, arrived, as_.at[d - 1], ar.at[d - 1], (row_peer(d), col)).wait_recv()
    for r in range(n_row):
        cross_ref[r * part:(r + 1) * part, :] = cfull[r]
    for copy in sends:
        copy.wait_send()
    for copy in stores:
        copy.wait()


def update_kernel(
    chunks, root_rows,
    factor_ref, inverse_ref, cross_ref, high_hbm, low_hbm, trail_hbm,
    rp_ref, rt_ref, basis_hbm, next_hbm,
    high, low, trail, basis, after,
    in_sem, out_sem,
):
    width = trail.shape[1] // chunks
    loads = []
    for k in range(chunks):
        window = pl.ds(k * width, width)
        loads.append([])
        for i, (src, dst) in enumerate(((high_hbm, high), (low_hbm, low), (trail_hbm, trail))):
            copy = pltpu.make_async_copy(src.at[:, window], dst.at[:, window], in_sem.at[k, i])
            copy.start()
            loads[k].append(copy)
    inverse = inverse_ref[...]
    count = inverse.shape[0]

    def exact(a, b):
        return jnp.dot(a, b, preferred_element_type=F32, precision=lax.Precision.HIGHEST)

    projected = exact(inverse, cross_ref[...])
    weights = exact(inverse.T, projected).T
    rp_ref[...] = factor_ref[...] * (1.0 / root_rows)
    rt_ref[...] = projected * (1.0 / root_rows)
    left_high, left_low = split(jnp.concatenate([inverse * root_rows, weights], axis=0))
    left = jnp.concatenate([left_high, left_low, left_high], axis=1)
    stores = []
    for k in range(chunks):
        window = pl.ds(k * width, width)
        for copy in loads[k]:
            copy.wait()
        p_high = high[:, window]
        result = dot(left, jnp.concatenate([p_high, p_high, low[:, window]], axis=0))
        basis[:, window] = result[:count]
        after[:, window] = trail[:, window] - result[count:]
        for i, (src, dst) in enumerate(((basis, basis_hbm), (after, next_hbm))):
            copy = pltpu.make_async_copy(src.at[:, window], dst.at[:, window], out_sem.at[k, i])
            copy.start()
            stores.append(copy)
    for copy in stores:
        copy.wait()


def solution(mesh):
    n_row, n_col = mesh.shape["row"], mesh.shape["col"]
    n_x = n_col // CORES
    chunks = len(PIECES)
    update_chunks = UPDATE_CHUNKS

    def on_device(candidates, trailing, pivots):
        cand_count, rows = candidates.shape
        tc = trailing.shape[0]
        count = pivots.shape[0]
        cap = count // 2
        eighth = rows // 8
        windows = tuple((sum(PIECES[:k]) * eighth, PIECES[k] * eighth) for k in range(chunks))
        part = count // n_row
        vmem = pl.BlockSpec(memory_space=pltpu.VMEM)
        hbm = pl.BlockSpec(memory_space=pl.ANY)
        dma = pltpu.SemaphoreType.DMA
        upper, inverse, cross, high, low = pl.pallas_call(
            functools.partial(gather_kernel, n_row, n_col, windows),
            name="gather",
            out_shape=(
                jax.ShapeDtypeStruct((count, count), F32),
                jax.ShapeDtypeStruct((count, count), F32),
                jax.ShapeDtypeStruct((count, tc), F32),
                jax.ShapeDtypeStruct((count, rows), BF16),
                jax.ShapeDtypeStruct((count, rows), BF16),
            ),
            in_specs=[vmem, hbm, hbm],
            out_specs=(vmem, vmem, vmem, hbm, hbm),
            scratch_shapes=[
                pltpu.VMEM((cand_count, rows), F32),
                pltpu.VMEM((tc, rows), F32),
                pltpu.VMEM((count, rows), BF16),
                pltpu.VMEM((count, rows), BF16),
                pltpu.VMEM((n_col, cap, rows), F32),
                pltpu.VMEM((n_row, count // 2, 2 * count), F32),
                pltpu.VMEM((n_row, part, tc), F32),
                pltpu.VMEM((n_row, part, tc), F32),
                pltpu.VMEM((n_row, part, tc), F32),
                dma((chunks,)), dma, dma((chunks, 2)),
                dma((chunks, n_x - 1)), dma((chunks, n_x - 1)),
                dma((chunks,)), dma((chunks,)),
                dma((chunks, n_x - 1)), dma((chunks, n_x - 1)),
                dma((n_row - 1,)), dma((n_row - 1,)),
                dma((n_row - 1,)), dma((n_row - 1,)),
                dma((n_row - 1,)), dma((n_row - 1,)),
            ] + [pltpu.SemaphoreType.REGULAR] * 3,
            compiler_params=pltpu.CompilerParams(collective_id=0, has_side_effects=True),
        )(pivots.reshape(1, count), candidates, trailing)
        root_rows = float(rows * n_row) ** 0.5
        return pl.pallas_call(
            functools.partial(update_kernel, update_chunks, root_rows),
            name="update",
            out_shape=(
                jax.ShapeDtypeStruct((count, count), F32),
                jax.ShapeDtypeStruct((count, tc), F32),
                jax.ShapeDtypeStruct((count, rows), F32),
                jax.ShapeDtypeStruct((tc, rows), F32),
            ),
            in_specs=[vmem, vmem, vmem, hbm, hbm, hbm],
            out_specs=(vmem, vmem, hbm, hbm),
            scratch_shapes=[
                pltpu.VMEM((count, rows), BF16),
                pltpu.VMEM((count, rows), BF16),
                pltpu.VMEM((tc, rows), F32),
                pltpu.VMEM((count, rows), F32),
                pltpu.VMEM((tc, rows), F32),
                dma((update_chunks, 3)), dma((update_chunks, 2)),
            ],
        )(upper, inverse, cross, high, low, trailing)

    placed = (P("col", "row"), P("col", "row"), P())
    return jax.shard_map(
        on_device,
        mesh=mesh,
        in_specs=placed,
        out_specs=(P(), P(None, "col"), P(None, "row"), P("col", "row")),
        check_vma=False,
    )
```

profile of v0, /device:TPU:0, one launch (start us, length us, event | category | flops | bytes accessed | tf_op | source)
XLA Modules:
  0.0 33.3 jit_solution(17023853836048108578)
XLA Ops:
  0.6 28.0 %gather.1 = (f32[64,64]{1,0:T(8,128)}, f32[64,64]{1,0:T(8,128)}, f32[64,128]{1,0:T(8,128)}, bf16[64,4096]{1,0:T(8,128)(2,1)}, bf16[64,4096]{1,0:T(8,128)(2,1)}) custom-call(s32[1,64]{1,0:T(1,128)} %bitcast.1, f32[128,4096]{1,0:T(8,128)} %cand_hbm.1, f32[128,4096]{1,0:T(8,128)} %trail_hbm.3), custom_call_target="tpu_custom_call" | custom-call | tf_op jit(solution)/shard_map/gather/pallas_call | solution.py:311
  28.6 4.7 %update.1 = (f32[64,64]{1,0:T(8,128)}, f32[64,128]{1,0:T(8,128)}, f32[64,4096]{1,0:T(8,128)}, f32[128,4096]{1,0:T(8,128)}) custom-call(f32[64,64]{1,0:T(8,128)} %get-tuple-element.9.factor_ref, f32[64,64]{1,0:T(8,128)} %get-tuple-element.10.inverse_ref, f32[64,128]{1,0:T(8,128)} %get-tuple-element.11.cross_ref, bf16[64,4096]{1,0:T(8,128)(2,1)} %get-tuple-element.12.high_hbm, ...), custom_call_target="tpu_custom_call" | custom-call | tf_op jit(solution)/shard_map/update/pallas_call | solution.py:344
where the time goes:
time: 33.6 us; the launch traced here: 33.3 us
  Pallas kernels  32.6 us (97%)
  between operations  0.64 us (2%)
    pallas_call x1, Pallas kernels, on_device(): pl.pallas_call(functools.partial(gather_kernel, n_row, n_col, windows), n...  28 us
    pallas_call x1, Pallas kernels, on_device(): pl.pallas_call(functools.partial(update_kernel, update_chunks, root_rows)...  4.66 us

commit v1 on v0

--- a/solution.py
+++ b/solution.py
@@ -14,6 +14,7 @@
 BLOCK = 16
 PIECES = (1, 4, 3)
 UPDATE_CHUNKS = 4
+GRANT = 24 * 2**20
 
 
 def split(x):
@@ -23,6 +24,10 @@
 
 def dot(a, b):
     return jnp.dot(a, b, preferred_element_type=F32)
+
+
+def exact(a, b):
+    return jnp.dot(a, b, preferred_element_type=F32, precision=lax.Precision.HIGHEST)
 
 
 def dot_t(a, b):
@@ -49,11 +54,11 @@
 
 
 def gather_kernel(
-    n_row, n_col, windows,
-    piv_ref, cand_hbm, trail_hbm,
-    factor_ref, inverse_ref, cross_ref, high_hbm, low_hbm,
-    cand, trail, high_ref, low_ref, bufs, grams, csend, crecv, cfull,
-    cand_sem, trail_sem, panel_sem,
+    n_row, n_col, windows, root_rows,
+    piv_hbm, cand_hbm, trail_hbm,
+    rp_ref, rt_ref, left_ref, high_ref, low_ref, trail,
+    piv_ref, cand, bufs, grams, csend, crecv, cfull,
+    piv_sem, cand_sem, trail_sem,
     xs, xr, ss, sr, fs, fr, gs, gr, cs, cr, as_, ar,
     up_sem, down_sem, mate_sem,
 ):
@@ -76,6 +81,8 @@
     def row_peer(d):
         return lax.rem(row + d, n_row)
 
+    piv_copy = pltpu.make_async_copy(piv_hbm, piv_ref, piv_sem)
+    piv_copy.start()
     cand_copies = []
     for k, (first, width) in enumerate(windows):
         window = pl.ds(first, width)
@@ -98,6 +105,7 @@
     pl.when(has_below)(lambda: signal(barrier, row - 2))
     pl.when(has_above)(lambda: signal(barrier, row + 2))
 
+    piv_copy.wait()
     piv_lane = jnp.broadcast_to(piv_ref[...].astype(F32), (count, count))
     rows_i, lanes_i = iota((count, count), 0), iota((count, count), 1)
     piv_sub = jnp.sum(jnp.where(rows_i == lanes_i, piv_lane, 0.0), axis=1, keepdims=True)
@@ -161,7 +169,6 @@
     signal(mate_sem, mate)
     tc = trail.shape[0]
     acc = jnp.zeros((count, count + tc), F32)
-    stores = []
     trail_copy.wait()
     for k, (first, width) in enumerate(windows):
         window = pl.ds(first, width)
@@ -182,10 +189,6 @@
         p_low = dot(expand, low).astype(BF16)
         high_ref[:, window] = p_high
         low_ref[:, window] = p_low
-        for i, (src, dst) in enumerate(((high_ref, high_hbm), (low_ref, low_hbm))):
-            copy = pltpu.make_async_copy(src.at[:, window], dst.at[:, window], panel_sem.at[k, i])
-            copy.start()
-            stores.append(copy)
         both = dot_t(jnp.concatenate([p_high, p_low], axis=0), jnp.concatenate([p_high, t_high], axis=0))
         acc += both[:count] + both[count:] + dot_t(p_high, jnp.concatenate([p_low, t_low], axis=0))
 
@@ -233,52 +236,38 @@
     wide = (count, 2 * count)
     diagonal = jnp.sum(jnp.where(iota(wide, 0) == iota(wide, 1), state, 0.0), axis=1, keepdims=True)
     scaled = state / jnp.sqrt(diagonal)
-    factor_ref[...] = jnp.where(iota(wide, 0) <= iota(wide, 1), scaled, 0.0)[:, :count]
-    inverse_ref[...] = scaled[:, count:]
+    factor = jnp.where(iota(wide, 0) <= iota(wide, 1), scaled, 0.0)[:, :count]
+    inverse = scaled[:, count:]
+    rp_ref[...] = factor * (1.0 / root_rows)
     for d in range(1, n_row):
         arrived = cfull.at[source(d)]
         remote(arrived, arrived, as_.at[d - 1], ar.at[d - 1], (row_peer(d), col)).wait_recv()
-    for r in range(n_row):
-        cross_ref[r * part:(r + 1) * part, :] = cfull[r]
+    projected = exact(inverse, cfull[...].reshape(count, tc))
+    weights = exact(inverse.T, projected).T
+    rt_ref[...] = projected * (1.0 / root_rows)
+    left_high, left_low = split(jnp.concatenate([inverse * root_rows, weights], axis=0))
+    left_ref[...] = jnp.concatenate([left_high, left_low, left_high], axis=1)
     for copy in sends:
         copy.wait_send()
-    for copy in stores:
-        copy.wait()
 
 
 def update_kernel(
-    chunks, root_rows,
-    factor_ref, inverse_ref, cross_ref, high_hbm, low_hbm, trail_hbm,
-    rp_ref, rt_ref, basis_hbm, next_hbm,
-    high, low, trail, basis, after,
-    in_sem, out_sem,
+    chunks,
+    rp_ref, rt_ref, left_ref, high, low, trail,
+    rp_hbm, rt_hbm, basis_hbm, next_hbm,
+    basis, after,
+    small_sem, out_sem,
 ):
+    stores = []
+    for i, (src, dst) in enumerate(((rp_ref, rp_hbm), (rt_ref, rt_hbm))):
+        copy = pltpu.make_async_copy(src, dst, small_sem.at[i])
+        copy.start()
+        stores.append(copy)
+    count = high.shape[0]
     width = trail.shape[1] // chunks
-    loads = []
+    left = left_ref[...]
     for k in range(chunks):
         window = pl.ds(k * width, width)
-        loads.append([])
-        for i, (src, dst) in enumerate(((high_hbm, high), (low_hbm, low), (trail_hbm, trail))):
-            copy = pltpu.make_async_copy(src.at[:, window], dst.at[:, window], in_sem.at[k, i])
-            copy.start()
-            loads[k].append(copy)
-    inverse = inverse_ref[...]
-    count = inverse.shape[0]
-
-    def exact(a, b):
-        return jnp.dot(a, b, preferred_element_type=F32, precision=lax.Precision.HIGHEST)
-
-    projected = exact(inverse, cross_ref[...])
-    weights = exact(inverse.T, projected).T
-    rp_ref[...] = factor_ref[...] * (1.0 / root_rows)
-    rt_ref[...] = projected * (1.0 / root_rows)
-    left_high, left_low = split(jnp.concatenate([inverse * root_rows, weights], axis=0))
-    left = jnp.concatenate([left_high, left_low, left_high], axis=1)
-    stores = []
-    for k in range(chunks):
-        window = pl.ds(k * width, width)
-        for copy in loads[k]:
-            copy.wait()
         p_high = high[:, window]
         result = dot(left, jnp.concatenate([p_high, p_high, low[:, window]], axis=0))
         basis[:, window] = result[:count]
@@ -306,31 +295,31 @@
         windows = tuple((sum(PIECES[:k]) * eighth, PIECES[k] * eighth) for k in range(chunks))
         part = count // n_row
         vmem = pl.BlockSpec(memory_space=pltpu.VMEM)
-        hbm = pl.BlockSpec(memory_space=pl.ANY)
+        hbm = pl.BlockSpec(memory_space=pltpu.HBM)
         dma = pltpu.SemaphoreType.DMA
-        upper, inverse, cross, high, low = pl.pallas_call(
-            functools.partial(gather_kernel, n_row, n_col, windows),
+        root_rows = float(rows * n_row) ** 0.5
+        handed = pl.pallas_call(
+            functools.partial(gather_kernel, n_row, n_col, windows, root_rows),
             name="gather",
             out_shape=(
                 jax.ShapeDtypeStruct((count, count), F32),
-                jax.ShapeDtypeStruct((count, count), F32),
                 jax.ShapeDtypeStruct((count, tc), F32),
+                jax.ShapeDtypeStruct((count + tc, 3 * count), BF16),
                 jax.ShapeDtypeStruct((count, rows), BF16),
                 jax.ShapeDtypeStruct((count, rows), BF16),
+                jax.ShapeDtypeStruct((tc, rows), F32),
             ),
-            in_specs=[vmem, hbm, hbm],
-            out_specs=(vmem, vmem, vmem, hbm, hbm),
+            in_specs=[hbm, hbm, hbm],
+            out_specs=(vmem,) * 6,
             scratch_shapes=[
+                pltpu.VMEM((1, count), jnp.int32),
                 pltpu.VMEM((cand_count, rows), F32),
-                pltpu.VMEM((tc, rows), F32),
-                pltpu.VMEM((count, rows), BF16),
-                pltpu.VMEM((count, rows), BF16),
                 pltpu.VMEM((n_col, cap, rows), F32),
                 pltpu.VMEM((n_row, count // 2, 2 * count), F32),
                 pltpu.VMEM((n_row, part, tc), F32),
                 pltpu.VMEM((n_row, part, tc), F32),
                 pltpu.VMEM((n_row, part, tc), F32),
-                dma((chunks,)), dma, dma((chunks, 2)),
+                dma, dma((chunks,)), dma,
                 dma((chunks, n_x - 1)), dma((chunks, n_x - 1)),
                 dma((chunks,)), dma((chunks,)),
                 dma((chunks, n_x - 1)), dma((chunks, n_x - 1)),
@@ -338,11 +327,12 @@
                 dma((n_row - 1,)), dma((n_row - 1,)),
                 dma((n_row - 1,)), dma((n_row - 1,)),
             ] + [pltpu.SemaphoreType.REGULAR] * 3,
-            compiler_params=pltpu.CompilerParams(collective_id=0, has_side_effects=True),
-        )(pivots.reshape(1, count), candidates, trailing)
-        root_rows = float(rows * n_row) ** 0.5
+            compiler_params=pltpu.CompilerParams(
+                collective_id=0, has_side_effects=True, vmem_limit_bytes=GRANT,
+            ),
+        )(*[pltpu.with_memory_space_constraint(a, pltpu.HBM) for a in (pivots.reshape(1, count), candidates, trailing)])
         return pl.pallas_call(
-            functools.partial(update_kernel, update_chunks, root_rows),
+            functools.partial(update_kernel, update_chunks),
             name="update",
             out_shape=(
                 jax.ShapeDtypeStruct((count, count), F32),
@@ -350,17 +340,15 @@
                 jax.ShapeDtypeStruct((count, rows), F32),
                 jax.ShapeDtypeStruct((tc, rows), F32),
             ),
-            in_specs=[vmem, vmem, vmem, hbm, hbm, hbm],
-            out_specs=(vmem, vmem, hbm, hbm),
+            in_specs=[vmem] * 6,
+            out_specs=(hbm,) * 4,
             scratch_shapes=[
-                pltpu.VMEM((count, rows), BF16),
-                pltpu.VMEM((count, rows), BF16),
-                pltpu.VMEM((tc, rows), F32),
                 pltpu.VMEM((count, rows), F32),
                 pltpu.VMEM((tc, rows), F32),
-                dma((update_chunks, 3)), dma((update_chunks, 2)),
+                dma((2,)), dma((update_chunks, 2)),
             ],
-        )(upper, inverse, cross, high, low, trailing)
+            compiler_params=pltpu.CompilerParams(vmem_limit_bytes=GRANT),
+        )(*handed)
 
     placed = (P("col", "row"), P("col", "row"), P())
     return jax.shard_map(

time: 33.6 us -> 30.3 us (0.902)
  Pallas kernels: 32.6 us -> 29.5 us
    pallas_call x2, Pallas kernels: 32.6 us -> 29.5 us  [the longest x1 27.5 us: on_device(): pl.pallas_call(functools.partial(gather_kernel, n_row, n_col, windows, ro...]
where the time goes in v1:
time: 30.3 us; the launch traced here: 30.1 us
  Pallas kernels  29.5 us (97%)
  between operations  0.64 us (2%)
    pallas_call x1, Pallas kernels, on_device(): pl.pallas_call(functools.partial(gather_kernel, n_row, n_col, windows, ro...  27.5 us
    pallas_call x1, Pallas kernels, on_device(): pl.pallas_call(functools.partial(update_kernel, update_chunks), name='upd...  1.98 us

profile of v1, /device:TPU:0, one launch (start us, length us, event | category | flops | bytes accessed | tf_op | source)
XLA Modules:
  0.0 30.1 jit_solution(17596982114285156953)
XLA Ops:
  0.6 27.5 %gather.1 = (f32[64,64]{1,0:T(8,128)S(1)}, f32[64,128]{1,0:T(8,128)S(1)}, bf16[192,192]{1,0:T(8,128)(2,1)S(1)}, bf16[64,4096]{1,0:T(8,128)(2,1)S(1)}, bf16[64,40...) custom-call(s32[1,64]{1,0:T(1,128)} %bitcast.1, f32[128,4096]{1,0:T(8,128)} %cand_hbm.1, f32[128,4096]{1,0:T(8,128)} %trail_hbm.1), custom_call_target="tpu_custom_call" | custom-call | tf_op jit(solution)/shard_map/gather/pallas_call | solution.py:301
  28.2 2.0 %update.1 = (f32[64,64]{1,0:T(8,128)}, f32[64,128]{1,0:T(8,128)}, f32[64,4096]{1,0:T(8,128)}, f32[128,4096]{1,0:T(8,128)}) custom-call(f32[64,64]{1,0:T(8,128)S(1)} %get-tuple-element.10.rp_ref, f32[64,128]{1,0:T(8,128)S(1)} %get-tuple-element.11.rt_ref, bf16[192,192]{1,0:T(8,128)(2,1)S(1)} %get-tuple-element.12.left_ref, ...), custom_call_target="tpu_custom_call" | custom-call | tf_op jit(solution)/shard_map/update/pallas_call | solution.py:334

commit v2 on v1

--- a/solution.py
+++ b/solution.py
@@ -54,12 +54,12 @@
 
 
 def gather_kernel(
-    n_row, n_col, windows, root_rows,
+    n_row, n_col, windows, root_rows, low, heavy,
     piv_hbm, cand_hbm, trail_hbm,
     rp_ref, rt_ref, left_ref, high_ref, low_ref, trail,
     piv_ref, cand, bufs, grams, csend, crecv, cfull,
     piv_sem, cand_sem, trail_sem,
-    xs, xr, ss, sr, fs, fr, gs, gr, cs, cr, as_, ar,
+    xs, xr, ss, sr, fs, fr, exs, exr, ess, esr, gs, gr, cs, cr, as_, ar,
     up_sem, down_sem, mate_sem,
 ):
     row = lax.axis_index("row")
@@ -69,8 +69,9 @@
     core = lax.rem(col, CORES)
     sibling = x * CORES + (1 - core)
     count = piv_ref.shape[1]
-    cap = count // 2
     cand_count = cand.shape[0]
+    slots = bufs.shape[0]
+    extra = pl.ds(n_col * low, slots - n_col * low)
 
     def x_peer(d):
         return lax.rem(x + d, n_x) * CORES + core
@@ -80,6 +81,20 @@
 
     def row_peer(d):
         return lax.rem(row + d, n_row)
+
+    barrier = pltpu.get_barrier_semaphore()
+    pl.semaphore_signal(barrier, inc=1, device_id=(row, sibling), device_id_type=MESH)
+    for d in range(1, n_x):
+        pl.semaphore_signal(barrier, inc=1, device_id=(row, x_peer(d)), device_id_type=MESH)
+    mate = row + 1 - 2 * lax.rem(row, 2)
+    has_below, has_above = row >= 2, row < n_row - 2
+
+    def signal(semaphore, to):
+        pl.semaphore_signal(semaphore, inc=1, device_id=(to, col), device_id_type=MESH)
+
+    signal(barrier, mate)
+    pl.when(has_below)(lambda: signal(barrier, row - 2))
+    pl.when(has_above)(lambda: signal(barrier, row + 2))
 
     piv_copy = pltpu.make_async_copy(piv_hbm, piv_ref, piv_sem)
     piv_copy.start()
@@ -90,20 +105,6 @@
         copy.start()
         cand_copies.append(copy)
     trail_copy = pltpu.make_async_copy(trail_hbm, trail, trail_sem)
-
-    barrier = pltpu.get_barrier_semaphore()
-    pl.semaphore_signal(barrier, inc=1, device_id=(row, sibling), device_id_type=MESH)
-    for d in range(1, n_x):
-        pl.semaphore_signal(barrier, inc=1, device_id=(row, x_peer(d)), device_id_type=MESH)
-    mate = row + 1 - 2 * lax.rem(row, 2)
-    has_below, has_above = row >= 2, row < n_row - 2
-
-    def signal(semaphore, to):
-        pl.semaphore_signal(semaphore, inc=1, device_id=(to, col), device_id_type=MESH)
-
-    signal(barrier, mate)
-    pl.when(has_below)(lambda: signal(barrier, row - 2))
-    pl.when(has_above)(lambda: signal(barrier, row + 2))
 
     piv_copy.wait()
     piv_lane = jnp.broadcast_to(piv_ref[...].astype(F32), (count, count))
@@ -117,10 +118,13 @@
     same = jnp.broadcast_to(owner_sub, (count, count)) == owner_lane
     rank_sub = jnp.sum(jnp.where(same & (lanes_i < rows_i), 1.0, 0.0), axis=1, keepdims=True)
     rank_lane = jnp.sum(jnp.where(same & (rows_i < lanes_i), 1.0, 0.0), axis=0, keepdims=True)
-    slot_sub = (owner_sub * cap + rank_sub).astype(jnp.int32)
-    slot_lane = (owner_lane[:1] * cap + rank_lane).astype(jnp.int32)
-    expand = (slot_sub == iota((count, n_col * cap), 1)).astype(F32).astype(BF16)
-    to_slot = (slot_lane == col * cap + iota((cap, count), 0)).astype(F32).astype(BF16)
+    def slot_of(owner, rank):
+        return jnp.where(rank < low, owner * low + rank, rank + (n_col - 1) * low).astype(jnp.int32)
+
+    expand = (slot_of(owner_sub, rank_sub) == iota((count, slots), 1)).astype(F32).astype(BF16)
+    own = iota((slots - (n_col - 1) * low, count), 0)
+    own = jnp.where(own < low, own + col * low, own + (n_col - 1) * low)
+    to_slot = (slot_of(owner_lane[:1], rank_lane) == own).astype(F32).astype(BF16)
     to_cand = (piv_sub.astype(jnp.int32) == col * cand_count + iota((count, cand_count), 1))
     pick = dot(to_slot, to_cand.astype(F32).astype(BF16)).astype(BF16)
 
@@ -130,19 +134,37 @@
             device_id=device, device_id_type=MESH,
         )
 
+    def mains(owner, window):
+        return bufs.at[pl.ds(pl.multiple_of(owner * low, low), low), window]
+
     sends = []
+    if heavy is not None:
+        heavy_x, heavy_core = heavy // CORES, heavy % CORES
+        is_heavy = col == heavy
+        is_relay = (core == heavy_core) & (x != heavy_x)
+        is_told = core == heavy_core
+
     for k, (first, width) in enumerate(windows):
         window = pl.ds(first, width)
         cand_copies[k].wait()
-        high, low = split(cand[:, window])
-        bufs[col, :, window] = dot(pick, high) + dot(pick, low)
+        high, low_part = split(cand[:, window])
+        picked = dot(pick, high) + dot(pick, low_part)
+        bufs[pl.ds(pl.multiple_of(col * low, low), low), window] = picked[:low]
         if k == 0:
             pl.semaphore_wait(barrier, n_x + 1 + has_below.astype(jnp.int32) + has_above.astype(jnp.int32))
-        mine = bufs.at[col, :, window]
+        mine = mains(col, window)
         for d in range(1, n_x):
             copy = remote(mine, mine, xs.at[k, d - 1], xr.at[k, d - 1], (row, x_peer(d)))
             copy.start()
             sends.append(copy)
+        if heavy is not None:
+            @pl.when(is_heavy)
+            def _():
+                bufs[extra, window] = picked[low:]
+                more = bufs.at[extra, window]
+                for d in range(1, n_x):
+                    remote(more, more, exs.at[k, d - 1], exr.at[k], (row, x_peer(d))).start()
+                remote(more, more, ess.at[k], esr.at[k], (row, sibling)).start()
         copy = remote(mine, mine, ss.at[k], sr.at[k], (row, sibling))
         copy.start()
         sends.append(copy)
@@ -170,27 +192,49 @@
     tc = trail.shape[0]
     acc = jnp.zeros((count, count + tc), F32)
     trail_copy.wait()
-    for k, (first, width) in enumerate(windows):
-        window = pl.ds(first, width)
+
+    def receive(k):
+        window = pl.ds(*windows[k])
         for d in range(1, n_x):
-            theirs = bufs.at[x_source(d), :, window]
+            theirs = mains(x_source(d), window)
             remote(theirs, theirs, xs.at[k, d - 1], xr.at[k, d - 1], (row, x_peer(d))).wait_recv()
             copy = remote(theirs, theirs, fs.at[k, d - 1], fr.at[k, d - 1], (row, sibling))
             copy.start()
             sends.append(copy)
+        if heavy is not None:
+            @pl.when(is_relay)
+            def _():
+                more = bufs.at[extra, window]
+                remote(more, more, exs.at[k, 0], exr.at[k], (row, x_peer(1))).wait_recv()
+                remote(more, more, ess.at[k], esr.at[k], (row, sibling)).start()
+
+    def gathered(k):
+        first, width = windows[k]
+        window = pl.ds(first, width)
         t_high, t_low = split(trail[:, window])
-        arrived = bufs.at[sibling, :, window]
+        arrived = mains(sibling, window)
         remote(arrived, arrived, ss.at[k], sr.at[k], (row, sibling)).wait_recv()
         for d in range(1, n_x):
-            arrived = bufs.at[lax.rem(x + n_x - d, n_x) * CORES + (1 - core), :, window]
+            arrived = mains(lax.rem(x + n_x - d, n_x) * CORES + (1 - core), window)
             remote(arrived, arrived, fs.at[k, d - 1], fr.at[k, d - 1], (row, sibling)).wait_recv()
-        high, low = split(bufs[:, :, window].reshape(n_col * cap, width))
+        if heavy is not None:
+            @pl.when(jnp.logical_not(is_told))
+            def _():
+                more = bufs.at[extra, window]
+                remote(more, more, ess.at[k], esr.at[k], (row, sibling)).wait_recv()
+        high, low_part = split(bufs[:, window])
         p_high = dot(expand, high).astype(BF16)
-        p_low = dot(expand, low).astype(BF16)
+        p_low = dot(expand, low_part).astype(BF16)
         high_ref[:, window] = p_high
         low_ref[:, window] = p_low
         both = dot_t(jnp.concatenate([p_high, p_low], axis=0), jnp.concatenate([p_high, t_high], axis=0))
-        acc += both[:count] + both[count:] + dot_t(p_high, jnp.concatenate([p_low, t_low], axis=0))
+        return both[:count] + both[count:] + dot_t(p_high, jnp.concatenate([p_low, t_low], axis=0))
+
+    for k in range(len(windows)):
+        receive(k)
+        if k > 0:
+            acc += gathered(k - 1)
+    acc += gathered(len(windows) - 1)
 
     pl.semaphore_wait(mate_sem, 1)
     part = count // n_row
@@ -249,6 +293,18 @@
     left_ref[...] = jnp.concatenate([left_high, left_low, left_high], axis=1)
     for copy in sends:
         copy.wait_send()
+    if heavy is not None:
+        for k, (first, width) in enumerate(windows):
+            more = bufs.at[extra, pl.ds(first, width)]
+
+            @pl.when(is_heavy)
+            def _():
+                for d in range(1, n_x):
+                    remote(more, more, exs.at[k, d - 1], exr.at[k], (row, x_peer(d))).wait_send()
+
+            @pl.when(is_told)
+            def _():
+                remote(more, more, ess.at[k], esr.at[k], (row, sibling)).wait_send()
 
 
 def update_kernel(
@@ -287,19 +343,40 @@
     update_chunks = UPDATE_CHUNKS
 
     def on_device(candidates, trailing, pivots):
+        count = pivots.shape[0]
+        cand_count = candidates.shape[0]
+        low = count // 4
+        owner = pivots // cand_count
+        index = jnp.int32(n_col)
+        ones = jnp.uint32(0)
+        for base in range(0, n_col, 4):
+            here = (owner >= base) & (owner < base + 4)
+            shift = (8 * (owner & 3)).astype(jnp.uint32)
+            held = jnp.sum(jnp.where(here, jnp.uint32(1) << shift, jnp.uint32(0)))
+            over = (held + jnp.uint32((127 - low) * 0x01010101)) & jnp.uint32(0x80808080)
+            for c in range(base, min(base + 4, n_col)):
+                alone = (over == jnp.uint32(0x80 << (8 * (c - base)))) & (ones == 0)
+                index = jnp.where(alone, c, index)
+            index = jnp.where((over != 0) & (ones != 0), n_col, index)
+            ones = ones | over
+        branches = [functools.partial(step, low, heavy) for heavy in range(n_col)]
+        branches.append(functools.partial(step, count // 2, None))
+        return lax.switch(index, branches, candidates, trailing, pivots)
+
+    def step(low, heavy, candidates, trailing, pivots):
         cand_count, rows = candidates.shape
         tc = trailing.shape[0]
         count = pivots.shape[0]
-        cap = count // 2
-        eighth = rows // 8
-        windows = tuple((sum(PIECES[:k]) * eighth, PIECES[k] * eighth) for k in range(chunks))
+        slots = n_col * low + (0 if heavy is None else count // 2 - low)
+        unit = rows // sum(PIECES)
+        windows = tuple((sum(PIECES[:k]) * unit, PIECES[k] * unit) for k in range(chunks))
         part = count // n_row
         vmem = pl.BlockSpec(memory_space=pltpu.VMEM)
         hbm = pl.BlockSpec(memory_space=pltpu.HBM)
         dma = pltpu.SemaphoreType.DMA
         root_rows = float(rows * n_row) ** 0.5
         handed = pl.pallas_call(
-            functools.partial(gather_kernel, n_row, n_col, windows, root_rows),
+            functools.partial(gather_kernel, n_row, n_col, windows, root_rows, low, heavy),
             name="gather",
             out_shape=(
                 jax.ShapeDtypeStruct((count, count), F32),
@@ -314,7 +391,7 @@
             scratch_shapes=[
                 pltpu.VMEM((1, count), jnp.int32),
                 pltpu.VMEM((cand_count, rows), F32),
-                pltpu.VMEM((n_col, cap, rows), F32),
+                pltpu.VMEM((slots, rows), F32),
                 pltpu.VMEM((n_row, count // 2, 2 * count), F32),
                 pltpu.VMEM((n_row, part, tc), F32),
                 pltpu.VMEM((n_row, part, tc), F32),
@@ -323,12 +400,13 @@
                 dma((chunks, n_x - 1)), dma((chunks, n_x - 1)),
                 dma((chunks,)), dma((chunks,)),
                 dma((chunks, n_x - 1)), dma((chunks, n_x - 1)),
+                dma((chunks, n_x - 1)), dma((chunks,)), dma((chunks,)), dma((chunks,)),
                 dma((n_row - 1,)), dma((n_row - 1,)),
                 dma((n_row - 1,)), dma((n_row - 1,)),
                 dma((n_row - 1,)), dma((n_row - 1,)),
             ] + [pltpu.SemaphoreType.REGULAR] * 3,
             compiler_params=pltpu.CompilerParams(
-                collective_id=0, has_side_effects=True, vmem_limit_bytes=GRANT,
+                collective_id=n_col if heavy is None else heavy, has_side_effects=True, vmem_limit_bytes=GRANT,
             ),
         )(*[pltpu.with_memory_space_constraint(a, pltpu.HBM) for a in (pivots.reshape(1, count), candidates, trailing)])
         return pl.pallas_call(

time: 30.3 us -> 31.3 us (1.033); the launches traced: 30.1 us -> 30.8 us
  Pallas kernels: 29.5 us -> 27.4 us
  other arithmetic: 0 us -> 1.3 us
  between operations: 0.64 us -> 1.5 us
  loops' own time: 0 us -> 0.53 us
    pallas_call x2, Pallas kernels: 29.5 us -> 27.4 us  [the longest x1 25.5 us: step(): pl.pallas_call(functools.partial(gather_kernel, n_row, n_col, windows, ro...]
    reduce_sum x0 -> x1, other arithmetic: none -> 1.3 us  [on_device(): held = jnp.sum(jnp.where(here, jnp.uint32(1) << shift, jnp.uint32(0)))]
    another operation x0 -> x1, loops' own time: none -> 0.53 us  [on_device(): return lax.switch(index, branches, candidates, trailing, pivots)]
where the time goes in v2:
time: 31.3 us; the launch traced here: 30.8 us
  Pallas kernels  27.4 us (88%)
  between operations  1.5 us (5%)
  other arithmetic  1.3 us (4%)
  loops' own time  0.53 us (2%)
    pallas_call x1, Pallas kernels, step(): pl.pallas_call(functools.partial(gather_kernel, n_row, n_col, windows, ro...  25.5 us
    pallas_call x1, Pallas kernels, step(): pl.pallas_call(functools.partial(update_kernel, update_chunks), name='upd...  1.98 us
    reduce_sum x1, other arithmetic, on_device(): held = jnp.sum(jnp.where(here, jnp.uint32(1) << shift, jnp.uint32(0)))  1.3 us

profile of v2, /device:TPU:0, one launch (start us, length us, event | category | flops | bytes accessed | tf_op | source)
XLA Modules:
  0.0 30.8 jit_solution(15002674504165197089)
XLA Ops:
  0.6 1.3 %fusion = u32[]{:T(128)} fusion(s32[64]{0:T(128)} %param.10), kind=kLoop, calls=%fused_computation.5 | loop fusion | flops 1535 | bytes 260 | tf_op jit(solution)/shard_map/reduce_sum | solution.py:355
  2.6 28.0 %conditional.1 = ((f32[64,64]{1,0:T(8,128)}, f32[64,128]{1,0:T(8,128)}, f32[64,4096]{1,0:T(8,128)}, f32[128,4096]{1,0:T(8,128)})) conditional(s32[]{:T(128)} %clamp.3, (s32[64]{0:T(128)}, f32[128,4096]{1,0:T(8,128)}, f32[128,4096]{1,0:T(8,128)}) %tuple.22, (s32[64]{0:T(128)}, f32[128,4096]{1,0:T(8,128)}, ...), branch_computations={%region_1.2_spmd, %region_2.3_spmd, %region_3.4_spmd, %region_4.5_... | conditional | bytes 8 | solution.py:364
  2.9 25.5 %gather.8 = (f32[64,64]{1,0:T(8,128)S(1)}, f32[64,128]{1,0:T(8,128)S(1)}, bf16[192,192]{1,0:T(8,128)(2,1)S(1)}, bf16[64,4096]{1,0:T(8,128)(2,1)S(1)}, bf16[64,40...) custom-call(s32[1,64]{1,0:T(1,128)} %bitcast.8, f32[128,4096]{1,0:T(8,128)} %get-tuple-element.58.cand_hbm, ...), custom_call_target="tpu_custom_call" | custom-call | tf_op jit(solution)/shard_map/cond/branch_3_fun/gather/pallas_call | solution.py:378
  28.3 2.0 %update.8 = (f32[64,64]{1,0:T(8,128)}, f32[64,128]{1,0:T(8,128)}, f32[64,4096]{1,0:T(8,128)}, f32[128,4096]{1,0:T(8,128)}) custom-call(f32[64,64]{1,0:T(8,128)S(1)} %get-tuple-element.60.rp_ref, f32[64,128]{1,0:T(8,128)S(1)} %get-tuple-element.61.rt_ref, bf16[192,192]{1,0:T(8,128)(2,1)S(1)} %get-tuple-element.62.left_ref, ...), custom_call_target="tpu_custom_call" | custom-call | tf_op jit(solution)/shard_map/cond/branch_3_fun/update/pallas_call | solution.py:412
